TPU v7x, 32 devices: a whole 2x2x4 slice. The times are simulated.
32 devices in a mesh: grp: 2 (over y), lon: 16 (over z, x, core).
Axes of the slice: x: 2, y: 2, z: 4, core: 2. Of those that a mesh axis runs over, the one named last changes fastest.
Arguments:
- base_state: bfloat16 [384, 6, 768], P(('grp', 'lon')), parts along dimension 0, may hold values from -6 to 6
- tangents: bfloat16 [2, 384, 6, 768], P(None, ('grp', 'lon')), parts along dimension 1, may hold values from -120 to 120
- norm_gain: float32 [192], replicated, may hold values from 0.25 to 1.75
- qkv_weight: bfloat16 [192, 576], replicated, may hold values from -0.4375 to 0.4375
- out_weight: bfloat16 [192, 192], replicated, may hold values from -0.4375 to 0.4375
- bias_table: float32 [2, 3312, 6], replicated, may hold values from -2 to 306
- bias_index: int32 [144, 144], replicated, may hold values from 0 to 3311
- region: int32 [6, 4], replicated, may hold values from 0 to 2
- energy_table: float32 [3, 192], replicated, may hold values from 0.3 to 3
- level_class: int32 [4], replicated, may hold values from 0 to 2
Outputs:
- singular: float32 [2, 384, 6, 768], P(None, ('grp', 'lon')), parts along dimension 1
There are 2 independent parts, one for each index of `grp`. A program takes and returns all parts, laid end to end along the dimension named above; an argument that names none is the same for every part. Nothing has to cross between parts.
All inputs are finite; a program needn't handle non-finite values.
Results may differ from a plain program's by a relative error of at most 0.015.
Values may be sent and summed in bfloat16 or wider, within the bound.
No kernel may reach another device: no remote copies, remote signals or barrier semaphores. Data moves between devices by JAX's collectives and lax.ppermute only.
A program may use at most 128 MiB of HBM per device.

v0:
```python
import functools

import jax
import jax.numpy as jnp
from jax import lax
from jax.experimental import pallas as pl
from jax.experimental.pallas import tpu as pltpu
from jax.sharding import PartitionSpec as P

C = 192
HEADS = 6
HEAD = 32
WLON = 12
WLAT = 6
WLEV = 2
LEV = 4
ECLS = 3
LAT = 6
WTYPES = 2
NPOS = 3312

HALF = WLON // 2
TOK = WLON * WLAT * WLEV
PLANE = WLON * WLAT
LANE = 128
TAIL = TOK - LANE
WIDE = 2 * LANE
KEYS = (HEADS + 1) * LANE
ROWS = -(-NPOS // LANE)
NEG = -1000000000.0


def iota(shape, dim):
    return lax.broadcasted_iota(jnp.int32, shape, dim)


def dot(a, b):
    return lax.dot_general(a, b, (((1,), (0,)), ((), ())), preferred_element_type=jnp.float32)


def dot_nt(a, b):
    return lax.dot_general(a, b, (((1,), (1,)), ((), ())), preferred_element_type=jnp.float32)


def dot_tn(a, b):
    return lax.dot_general(a, b, (((0,), (0,)), ((), ())), preferred_element_type=jnp.float32)


def bias_kernel(region, idx_ref, tab_ref, out_ref, hi_ref, lo_ref):
    row, col = iota((TOK, TOK), 0), iota((TOK, TOK), 1)
    rows = ((row % PLANE) * WLEV + row // PLANE == col).astype(jnp.bfloat16)
    row, col = iota((TOK, WIDE), 0), iota((TOK, WIDE), 1)
    key = jnp.where(col < LANE, col, LANE + col % TAIL)
    cols = ((key % PLANE) * WLEV + key // PLANE == row).astype(jnp.bfloat16)

    def ordered(value):
        value = value.astype(jnp.float32).astype(jnp.bfloat16)
        return dot(dot(rows, value).astype(jnp.bfloat16), cols).astype(jnp.int32)

    idx = idx_ref[...]
    high, low = ordered(idx >> 7), ordered(idx & 127)
    hi_ref[0:TOK, :] = high[:, :LANE]
    lo_ref[0:TOK, :] = low[:, :LANE]
    slot = iota((8, LANE), 1) // TAIL
    for pack in range(-(-TOK // 64)):
        h = jnp.zeros((8, LANE), jnp.int32)
        l = jnp.zeros((8, LANE), jnp.int32)
        for u in range(8):
            at = 64 * pack + 8 * u
            if at < TOK:
                h = jnp.where(slot == u, high[at : at + 8, LANE:], h)
                l = jnp.where(slot == u, low[at : at + 8, LANE:], l)
        hi_ref[TOK + 8 * pack : TOK + 8 * pack + 8, :] = h
        lo_ref[TOK + 8 * pack : TOK + 8 * pack + 8, :] = l

    def gathered(at):
        h, l = hi_ref[pl.ds(at, 8), :], lo_ref[pl.ds(at, 8), :]
        found = [jnp.zeros((8, LANE), jnp.float32) for _ in range(WTYPES * HEADS)]
        for b in range(ROWS):
            here = h == b
            for n in range(WTYPES * HEADS):
                source = jnp.broadcast_to(tab_ref[n, b : b + 1, :], (8, LANE))
                found[n] = jnp.where(here, jnp.take_along_axis(source, l, axis=1), found[n])
        return found

    def regions(token, t):
        level, lat = token // PLANE, token % WLAT
        found = jnp.zeros(token.shape, jnp.int32)
        for l in range(WLEV):
            for j in range(WLAT):
                found = jnp.where((level == l) & (lat == j), region[j, WLEV * t + l], found)
        return found

    lane = iota((8, LANE), 1)
    key_main = [regions(lane, t) for t in range(WTYPES)]
    key_tail = [regions(LANE + lane % TAIL, t) for t in range(WTYPES)]

    def main_rows(g, _):
        at = pl.multiple_of(g * 8, 8)
        found = gathered(at)
        query = iota((8, LANE), 0) + at
        for t in range(WTYPES):
            ok = regions(query, t) == key_main[t]
            for h in range(HEADS):
                out_ref[t, pl.ds(at, 8), LANE * h : LANE * (h + 1)] = jnp.where(ok, found[t * HEADS + h], NEG)
        return 0

    lax.fori_loop(0, TOK // 8, main_rows, 0)
    for pack in range(-(-TOK // 64)):
        found = gathered(TOK + 8 * pack)
        for u in range(8):
            at = 64 * pack + 8 * u
            if at >= TOK:
                break
            query = iota((8, LANE), 0) + at
            for t in range(WTYPES):
                ok = (regions(query, t) == key_tail[t]) & (slot < HEADS)
                value = jnp.full((8, LANE), NEG, jnp.float32)
                for h in range(HEADS):
                    moved = pltpu.roll(found[t * HEADS + h], (TAIL * (h - u)) % LANE, 1)
                    value = jnp.where(slot == h, moved, value)
                out_ref[t, at : at + 8, LANE * HEADS :] = jnp.where(ok, value, NEG)


def window_kernel(classes, x_ref, gain_ref, w_ref, out_w_ref, bias_ref, table_ref, scaled_ref, sums_ref):
    f32, bf16 = jnp.float32, jnp.bfloat16
    gain = gain_ref[...]
    wq, wk, wv = (w_ref[:, WIDE * n : WIDE * (n + 1)] for n in range(3))
    wo = out_w_ref[...]
    scale = HEAD ** (-0.5)
    table = table_ref[...]

    def energy_row(level):
        found = jnp.zeros((1, C), f32)
        for e in range(ECLS):
            found = found + jnp.where(classes[level] == e, table[e : e + 1, :], 0.0)
        return found

    lane = iota((1, WIDE), 1)
    head_of = jnp.where(lane < C, lane // HEAD, -1)
    row, col = iota((WIDE, WIDE), 0), iota((WIDE, WIDE), 1)
    spread = ((row < C) & (col >= C) & ((col - C) % 32 == row // HEAD)).astype(bf16)

    def by_head(value, ones):
        main, tail = [], []
        for h in range(HEADS):
            keep = head_of == h
            rest = jnp.zeros((1, WIDE), bf16)
            if ones:
                rest = ((lane == C + h) | (lane == C + 32 + h)).astype(bf16)
            main.append(jnp.where(keep, value[:LANE], rest))
            tail.append(jnp.where(keep, value[LANE:], rest))
        filler = jnp.zeros((KEYS - HEADS * TOK, WIDE), bf16)
        return jnp.concatenate(main + tail + [filler], 0)

    def with_shift(value, product):
        high = product.astype(bf16)
        low = (product - high.astype(f32)).astype(bf16)
        sums = dot(high, spread) + dot(low, spread)
        top = sums.astype(bf16)
        rest = (sums - top.astype(f32)).astype(bf16)
        return jnp.where(lane < C, value, jnp.where(lane < C + 32, -top, -rest))

    def transposed_product(left_t, ds):
        main = []
        for j in range(HEADS // 2):
            part = dot(left_t[64 * j : 64 * j + 64], ds[:, WIDE * j : WIDE * (j + 1)])
            main += [part[:HEAD, :LANE], part[HEAD:, LANE:]]
        last = dot(left_t[:C], ds[:, LANE * HEADS :])
        tail = []
        for h in range(HEADS):
            block = last[HEAD * h : HEAD * (h + 1)]
            tail.append(pltpu.roll(block, (LANE - TAIL * h) % LANE, 1)[:, :TAIL])
        return jnp.concatenate([jnp.concatenate(main, 0), jnp.concatenate(tail, 0)], 1)

    slot = iota((TOK, LANE), 1) // TAIL
    totals = [jnp.zeros((1, C), f32) for _ in range(3)]
    for t in range(WTYPES):
        def tokens(field):
            parts = [
                x_ref[0, field, :, C * l : C * (l + 1)].astype(f32)
                for l in range(WLEV * t, WLEV * (t + 1))
            ]
            return jnp.concatenate(parts, 0)

        base = tokens(0)
        centered = base - jnp.mean(base, -1, keepdims=True)
        rstd = lax.rsqrt(jnp.mean(centered * centered, -1, keepdims=True) + 1e-05)
        hat = centered * rstd
        normed = (hat * gain).astype(bf16)
        q, k, v = (dot(normed, w).astype(bf16) for w in (wq, wk, wv))
        k_heads, v_heads = by_head(k, True), by_head(v, True)

        scores = dot_nt(q, k_heads) * scale + bias_ref[t]
        tails = scores[:, LANE * HEADS :]
        raised, sums = [], []
        tail_peak = jnp.zeros((TOK, LANE), f32)
        for h in range(HEADS):
            main = scores[:, LANE * h : LANE * (h + 1)]
            peak = jnp.max(jnp.maximum(main, jnp.where(slot == h, tails, -jnp.inf)), -1, keepdims=True)
            raised.append(jnp.exp(main - peak))
            tail_peak = jnp.where(slot == h, peak, tail_peak)
        tails = jnp.exp(tails - tail_peak)
        tail_inv = jnp.zeros((TOK, LANE), f32)
        for h in range(HEADS):
            inv = 1.0 / jnp.sum(raised[h] + jnp.where(slot == h, tails, 0.0), -1, keepdims=True)
            raised[h] = raised[h] * inv
            tail_inv = jnp.where(slot == h, inv, tail_inv)
        probs = jnp.concatenate(raised + [tails * tail_inv], 1)
        weights = probs.astype(bf16)
        probs = probs * scale
        mean_v = dot(weights, v_heads)
        mean_k = dot(weights, k_heads)
        q_t = q.astype(f32).T.astype(bf16)

        def energy_rows():
            rows = [energy_row(WLEV * t + l) for l in range(WLEV)]
            return jnp.concatenate([jnp.broadcast_to(r, (PLANE, C)) for r in rows], 0)

        energy = energy_rows()
        result = []
        for f in range(2):
            direction = tokens(1 + f)
            moved = direction - jnp.mean(direction, -1, keepdims=True) - hat * jnp.mean(hat * direction, -1, keepdims=True)
            moved = (moved * rstd * gain).astype(bf16)
            dq, dk, dv = (dot(moved, w).astype(bf16) for w in (wq, wk, wv))
            dk_heads, dv_heads = by_head(dk, False), by_head(dv, False)
            mean_dk = dot(weights, dk_heads)
            mean_dv = dot(weights, dv_heads)
            shifted = with_shift(dq, dq.astype(f32) * mean_k + q.astype(f32) * mean_dk)
            dscores = dot_nt(shifted, k_heads) + dot_nt(q, dk_heads)
            dweights = (probs * dscores).astype(bf16)
            dblended = (dot(dweights, v_heads) + mean_dv).astype(bf16)
            image = direction + dot(dblended[:, :C], wo)

            cot = dot_nt((energy * image).astype(bf16), wo).astype(bf16)
            cot = jnp.concatenate([cot, jnp.zeros((TOK, WIDE - C), bf16)], 1)
            shifted = with_shift(cot, cot.astype(f32) * mean_v)
            cscores = (probs * dot_nt(shifted, v_heads)).astype(bf16)
            cq = dot(cscores, k_heads).astype(bf16)
            ck_t = transposed_product(q_t, cscores).astype(bf16)
            cv_t = transposed_product(cot.astype(f32).T.astype(bf16), weights).astype(bf16)
            cnormed = dot_nt(cq, wq) + dot_tn(ck_t, wk.T[:C]) + dot_tn(cv_t, wv.T[:C])
            cnormed = cnormed.astype(bf16).astype(f32) * gain
            back = cnormed - jnp.mean(cnormed, -1, keepdims=True) - hat * jnp.mean(hat * cnormed, -1, keepdims=True)
            out = image + back * rstd / energy
            result.append(out)
            for l in range(WLEV):
                at = WLEV * t + l
                scaled_ref[0, f, :, C * at : C * (at + 1)] = out[PLANE * l : PLANE * (l + 1)]
        for n, (a, b) in enumerate(((0, 0), (0, 1), (1, 1))):
            totals[n] = totals[n] + jnp.sum(energy * result[a] * result[b], 0, keepdims=True)
    lane = iota((1, LANE), 1)
    found = jnp.zeros((1, LANE), f32)
    for n in range(3):
        found = jnp.where(lane == n, jnp.sum(totals[n], -1, keepdims=True), found)
    sums_ref[0] = jnp.broadcast_to(found, (8, LANE))


def whole(memory=pltpu.VMEM):
    return pl.BlockSpec(memory_space=memory)


def pair_bias(bias_table, bias_index, region):
    table = jnp.transpose(bias_table, (0, 2, 1)).reshape(WTYPES * HEADS, NPOS)
    table = jnp.pad(table, ((0, 0), (0, ROWS * LANE - NPOS))).reshape(WTYPES * HEADS, ROWS, LANE)
    packs = TOK + 8 * -(-TOK // 64)
    return pl.pallas_call(
        bias_kernel,
        out_shape=jax.ShapeDtypeStruct((WTYPES, TOK, KEYS), jnp.float32),
        in_specs=[whole(pltpu.SMEM), whole(), whole()],
        out_specs=whole(),
        scratch_shapes=[pltpu.VMEM((packs, LANE), jnp.int32)] * 2,
        cost_estimate=pl.CostEstimate(flops=100000000, bytes_accessed=1400000, transcendentals=0),
        name="pair_bias",
    )(region, bias_index, table)


def windows(fields, gain, weight, out_weight, bias, energy_table, level_class):
    count = fields.shape[0]

    def fixed(shape):
        return pl.BlockSpec(shape, lambda n: (0,) * len(shape))

    def moving(shape):
        return pl.BlockSpec((1,) + shape[1:], lambda n: (n,) + (0,) * (len(shape) - 1))

    outs = [(count, 2, PLANE, LEV * C), (count, 8, LANE)]
    return pl.pallas_call(
        window_kernel,
        grid=(count,),
        out_shape=[jax.ShapeDtypeStruct(s, jnp.float32) for s in outs],
        in_specs=[
            whole(pltpu.SMEM),
            moving(fields.shape),
            fixed(gain.shape),
            fixed(weight.shape),
            fixed(out_weight.shape),
            fixed(bias.shape),
            fixed(energy_table.shape),
        ],
        out_specs=[moving(s) for s in outs],
        compiler_params=pltpu.CompilerParams(vmem_limit_bytes=48 * 1024 * 1024),
        cost_estimate=pl.CostEstimate(flops=2000000000, bytes_accessed=2500000, transcendentals=250000),
        name="window_step",
    )(level_class, fields, gain, weight, out_weight, bias, energy_table)


def summed(value, axis):
    size = lax.axis_size(axis)
    if size & (size - 1):
        return lax.psum(value, axis)
    step = 1
    while step < size:
        value = value + lax.ppermute(value, axis, [(i, i ^ step) for i in range(size)])
        step *= 2
    return value


def local(
    base_state,
    tangents,
    norm_gain,
    qkv_weight,
    out_weight,
    bias_table,
    bias_index,
    region,
    energy_table,
    level_class,
):
    columns = base_state.shape[0]
    size = lax.axis_size("lon")
    count = columns // WLON
    up = [(i, (i + 1) % size) for i in range(size)]
    down = [(j, i) for i, j in up]
    fields = jnp.concatenate([base_state[None], tangents], 0).reshape(3, columns * LAT, LEV * C)
    edge = HALF * LAT
    arrived = lax.ppermute(fields[:, :edge], "lon", down)
    bias = pair_bias(bias_table, bias_index, region)
    weight = jnp.pad(qkv_weight.reshape(C, 3, C), ((0, 0), (0, 0), (0, WIDE - C))).reshape(C, 3 * WIDE)
    shifted = jnp.concatenate([fields[:, edge:], arrived], 1)
    shifted = shifted.reshape(3, count, PLANE, LEV * C).swapaxes(0, 1)
    scaled, sums = windows(shifted, norm_gain[None], weight, out_weight, bias, energy_table, level_class)
    scaled = scaled.swapaxes(0, 1).reshape(2, columns * LAT, LEV * C)
    entries = jnp.sum(sums[:, 0, :], 0)
    kept = columns * LAT - edge
    returned = lax.ppermute(scaled[:, kept:].astype(jnp.bfloat16), "lon", up)
    entries = summed(entries, "lon")
    scaled = jnp.concatenate([returned.astype(jnp.float32), scaled[:, :kept]], 1)
    scaled = scaled.reshape(2, columns, LAT, LEV * C)
    total = float(columns * size * LAT * LEV * C)
    first = scaled[0] * jnp.sqrt(total / entries[0])
    second = scaled[1] - entries[1] / entries[0] * scaled[0]
    second_sum = entries[2] - entries[1] * entries[1] / entries[0]
    return jnp.stack([first, second * jnp.sqrt(total / second_sum)])


def solution(mesh):
    placed = (
        P(("grp", "lon"), None, None),
        P(None, ("grp", "lon"), None, None),
    ) + (P(),) * 8
    return jax.shard_map(
        local,
        mesh=mesh,
        in_specs=placed,
        out_specs=P(None, ("grp", "lon"), None, None),
        check_vma=False,
    )
```

profile of v0, /device:TPU:0, one launch (start us, length us, event | category | flops | bytes accessed | tf_op | source)
XLA Modules:
  0.0 52.7 jit_solution(2594410083853469619)
XLA Ops:
  0.0 0.0 copy-start.6
  0.0 1.0 %concatenate.14 = bf16[1,72,768]{2,1,0:T(8,128)(2,1)S(1)} reshape(bf16[12,6,768]{2,1,0:T(8,128)(2,1)} %param.10) | data formatting | bytes 221184 | tf_op jit(solution)/shard_map/concatenate | solution.py:337
  1.0 0.0 copy-done.6
  1.1 0.0 copy-start.8
  1.1 0.0 copy-start.7
  1.1 5.5 %collective-permute-start = (bf16[3,36,768]{2,1,0:T(8,128)(2,1)S(1)}, bf16[3,36,768]{2,1,0:T(8,128)(2,1)S(1)}, u32[]{:S(2)}, u32[]{:S(2)}) collective-permute-start(bf16[3,36,768]{2,1,0:T(8,128)(2,1)S(1)} %get-tuple-element.12), channel_id=1, source_target_pairs={{1,0},{2,1},{3,2},{4,3},{5,4},{6,5},{7,6},{8,7},{9,8},{10,9},{11,1... | collective-permute-start | bytes 497672 | tf_op jit(solution)/shard_map/ppermute | solution.py:339
  6.6 0.0 copy-done.8
  6.6 0.7 %copy.19.region = s32[6,4]{1,0:T(8,128)} copy(s32[6,4]{0,1:T(4,128)S(1)} %copy-done.8) | data formatting | bytes 192 | tf_op args[7]
  7.3 0.0 copy-done.7
  7.4 0.0 copy-start.5
  7.4 0.7 %reshape.66.tab_ref = f32[12,26,128]{2,1,0:T(8,128)} reshape(f32[12,3328]{1,0:T(8,128)S(1)} %pad.9) | data formatting | bytes 319488 | tf_op jit(solution)/shard_map/reshape | solution.py:266
  8.1 0.3 copy-done.5
  8.4 0.2 copy.16
  8.6 0.2 copy.20.w_ref
  8.8 11.0 %pair_bias.1.bias_ref = f32[2,144,896]{2,1,0:T(8,128)} custom-call(s32[6,4]{1,0:T(8,128)} %copy.19.region, s32[144,144]{1,0:T(8,128)} %idx_ref.1, f32[12,26,128]{2,1,0:T(8,128)} %reshape.66.tab_ref), custom_call_target="tpu_custom_call" | custom-call | flops 100000000 | bytes 1400000 | tf_op jit(solution)/shard_map/pair_bias/pallas_call | solution.py:268
  19.8 0.0 collective-permute-done
  19.8 0.0 copy-start.1
  19.8 0.0 copy-start.2
  19.8 0.1 maximum_bitcast_fusion.x_ref
  19.9 0.0 copy-start.3
  19.9 0.0 copy-start.4
  19.9 0.8 %copy-done.1 = bf16[192,192]{1,0:T(8,128)(2,1)S(1)} copy-done((bf16[192,192]{1,0:T(8,128)(2,1)S(1)}, bf16[192,192]{1,0:T(8,128)(2,1)}, u32[]{:S(2)}) %copy-start.1) | copy-done | bytes 73752
  20.7 0.0 copy-done.2
  20.7 0.0 copy-done.3
  20.7 0.0 copy-done.4
  20.7 0.0 copy-start
  20.7 1.2 %copy-done = f32[2,144,896]{2,1,0:T(8,128)S(1)} copy-done((f32[2,144,896]{2,1,0:T(8,128)S(1)}, f32[2,144,896]{2,1,0:T(8,128)}, u32[]{:S(2)}) %copy-start) | copy-done | bytes 1032216
  22.0 10.5 %window_step.1 = (f32[1,2,72,768]{3,2,1,0:T(8,128)S(1)}, f32[1,8,128]{2,1,0:T(8,128)S(1)}) custom-call(s32[4]{0:T(128)S(1)} %copy-done.4, bf16[1,3,72,768]{3,2,1,0:T(8,128)(2,1)S(1)} %maximum_bitcast_fusion.x_ref, f32[1,192]{1,0:T(1,128)S(1)} %bitcast.17, bf16[192,768]{1,0:T(8,128)(2,1)S(1)} %copy.20.w_ref, bf16[192,192]{1,0:T(8,128)(2,1)S(1)} %copy-done.1, ...), custom_call_target="tpu_custom_call" | custom-call | flops 2000000000 | bytes 2500000 | tf_op jit(solution)/shard_map/window_step/pallas_call | solution.py:289
  32.5 0.1 collective-permute-start.2
  32.6 1.1 %collective-permute-done.2 = f32[128]{0:T(128)S(1)} collective-permute-done((f32[128]{0:T(128)S(1)}, f32[128]{0:T(128)S(1)}, u32[]{:S(2)}, u32[]{:S(2)}) %collective-permute-start.2) | collective-permute-done | bytes 544 | tf_op jit(solution)/shard_map/ppermute | solution.py:315
  33.7 0.0 collective-permute-start.3
  33.7 3.6 %collective-permute-done.3 = f32[128]{0:T(128)S(1)} collective-permute-done((f32[128]{0:T(128)S(1)}, f32[128]{0:T(128)S(1)}, u32[]{:S(2)}, u32[]{:S(2)}) %collective-permute-start.3) | collective-permute-done | bytes 544 | tf_op jit(solution)/shard_map/ppermute | solution.py:315
  37.3 0.0 collective-permute-start.4
  37.3 3.6 %collective-permute-done.4 = f32[128]{0:T(128)S(1)} collective-permute-done((f32[128]{0:T(128)S(1)}, f32[128]{0:T(128)S(1)}, u32[]{:S(2)}, u32[]{:S(2)}) %collective-permute-start.4) | collective-permute-done | bytes 544 | tf_op jit(solution)/shard_map/ppermute | solution.py:315
  40.9 0.0 collective-permute-start.5
  40.9 0.1 collective-permute-start.1
  41.0 4.3 %collective-permute-done.5 = f32[128]{0:T(128)S(1)} collective-permute-done((f32[128]{0:T(128)S(1)}, f32[128]{0:T(128)S(1)}, u32[]{:S(2)}, u32[]{:S(2)}) %collective-permute-start.5) | collective-permute-done | bytes 544 | tf_op jit(solution)/shard_map/ppermute | solution.py:315
  45.3 0.7 %fusion.5 = (f32[1]{0:T(128)}, f32[1]{0:T(128)}, f32[1]{0:T(128)}) fusion(f32[128]{0:T(128)S(1)} %add.19), kind=kLoop, calls=%fused_computation.15 | loop fusion | bytes 24 | tf_op jit(solution)/shard_map/slice | solution.py:353
  50.9 0.0 collective-permute-done.1
  51.0 0.1 broadcast_multiply_fusion
  51.1 0.2 mul.51
  51.3 0.2 mul.57
  51.5 1.2 %pad_maximum_fusion = f32[2,12,6,768]{3,0,2,1:T(2,128)} fusion(f32[1,12,6,768]{3,0,2,1:T(1,128)S(1)} %mul.57, f32[1,12,6,768]{3,0,2,1:T(1,128)S(1)} %mul.51), kind=kLoop, calls=%fused_computation.2 | loop fusion | flops 110592 | bytes 884736 | tf_op jit(solution)/shard_map/stack | solution.py:356
  (15 shorter events, 0.3 us)
Async XLA Ops:
  0.0 1.0 %copy-start.6 = (bf16[2,12,6,768]{3,0,2,1:T(2,128)(2,1)S(1)}, bf16[2,12,6,768]{3,0,2,1:T(2,128)(2,1)}, u32[]{:S(2)}) copy-start(bf16[2,12,6,768]{3,0,2,1:T(2,128)(2,1)} %param.11) | copy-start | bytes 663556
  1.1 5.6 %copy-start.8 = (s32[6,4]{0,1:T(4,128)S(1)}, s32[6,4]{0,1:T(4,128)}, u32[]{:S(2)}) copy-start(s32[6,4]{0,1:T(4,128)} %param.17) | copy-start | bytes 292
  1.1 6.2 %copy-start.7 = (f32[2,3312,6]{1,0,2:T(2,128)S(1)}, f32[2,3312,6]{1,0,2:T(2,128)}, u32[]{:S(2)}) copy-start(f32[2,3312,6]{1,0,2:T(2,128)} %param.15) | copy-start | bytes 476932
  1.1 18.7 %collective-permute-start = (bf16[3,36,768]{2,1,0:T(8,128)(2,1)S(1)}, bf16[3,36,768]{2,1,0:T(8,128)(2,1)S(1)}, u32[]{:S(2)}, u32[]{:S(2)}) collective-permute-start(bf16[3,36,768]{2,1,0:T(8,128)(2,1)S(1)} %get-tuple-element.12), channel_id=1, source_target_pairs={{1,0},{2,1},{3,2},{4,3},{5,4},{6,5},{7,6},{8,7},{9,8},{10,9},{11,1... | collective-permute-start | bytes 497672 | tf_op jit(solution)/shard_map/ppermute | solution.py:339
  7.4 1.0 %copy-start.5 = (bf16[192,576]{1,0:T(8,128)(2,1)S(1)}, bf16[192,576]{1,0:T(8,128)(2,1)}, u32[]{:S(2)}) copy-start(bf16[192,576]{1,0:T(8,128)(2,1)} %param.13) | copy-start | bytes 663556
  19.8 0.9 %copy-start.1 = (bf16[192,192]{1,0:T(8,128)(2,1)S(1)}, bf16[192,192]{1,0:T(8,128)(2,1)}, u32[]{:S(2)}) copy-start(bf16[192,192]{1,0:T(8,128)(2,1)} %out_w_ref.1) | copy-start | bytes 221188
  19.8 0.9 %copy-start.2 = (f32[3,192]{1,0:T(4,128)S(1)}, f32[3,192]{1,0:T(4,128)}, u32[]{:S(2)}) copy-start(f32[3,192]{1,0:T(4,128)} %table_ref.1) | copy-start | bytes 6916
  19.9 0.8 %copy-start.3 = (f32[192]{0:T(256)S(1)}, f32[192]{0:T(256)}, u32[]{:S(2)}) copy-start(f32[192]{0:T(256)} %param.12) | copy-start | bytes 2308
  19.9 0.8 %copy-start.4 = (s32[4]{0:T(128)S(1)}, s32[4]{0:T(128)}, u32[]{:S(2)}) copy-start(s32[4]{0:T(128)} %classes.1) | copy-start | bytes 52
  20.7 1.2 %copy-start = (f32[2,144,896]{2,1,0:T(8,128)S(1)}, f32[2,144,896]{2,1,0:T(8,128)}, u32[]{:S(2)}) copy-start(f32[2,144,896]{2,1,0:T(8,128)} %pair_bias.1.bias_ref) | copy-start | bytes 3096580
  32.5 1.2 %collective-permute-start.2 = (f32[128]{0:T(128)S(1)}, f32[128]{0:T(128)S(1)}, u32[]{:S(2)}, u32[]{:S(2)}) collective-permute-start(f32[128]{0:T(128)S(1)} %slice_bitcast_fusion), channel_id=1, source_target_pairs={{0,1},{1,0},{2,3},{3,2},{4,5},{5,4},{6,7},{7,6},{8,9},{9,8},{10,11... | collective-permute-start | bytes 1544 | tf_op jit(solution)/shard_map/ppermute | solution.py:315
  33.7 3.6 %collective-permute-start.3 = (f32[128]{0:T(128)S(1)}, f32[128]{0:T(128)S(1)}, u32[]{:S(2)}, u32[]{:S(2)}) collective-permute-start(f32[128]{0:T(128)S(1)} %fusion.3), channel_id=1, source_target_pairs={{0,2},{1,3},{2,0},{3,1},{4,6},{5,7},{6,4},{7,5},{8,10},{9,11},{10,... | collective-permute-start | bytes 1544 | tf_op jit(solution)/shard_map/ppermute | solution.py:315
  37.3 3.6 %collective-permute-start.4 = (f32[128]{0:T(128)S(1)}, f32[128]{0:T(128)S(1)}, u32[]{:S(2)}, u32[]{:S(2)}) collective-permute-start(f32[128]{0:T(128)S(1)} %add.17), channel_id=1, source_target_pairs={{0,4},{1,5},{2,6},{3,7},{4,0},{5,1},{6,2},{7,3},{8,12},{9,13},{10,... | collective-permute-start | bytes 1544 | tf_op jit(solution)/shard_map/ppermute | solution.py:315
  40.9 4.5 %collective-permute-start.5 = (f32[128]{0:T(128)S(1)}, f32[128]{0:T(128)S(1)}, u32[]{:S(2)}, u32[]{:S(2)}) collective-permute-start(f32[128]{0:T(128)S(1)} %add.18), channel_id=1, source_target_pairs={{0,8},{1,9},{2,10},{3,11},{4,12},{5,13},{6,14},{7,15},{8,0},{9,1},... | collective-permute-start | bytes 1544 | tf_op jit(solution)/shard_map/ppermute | solution.py:315
  40.9 10.0 %collective-permute-start.1 = (bf16[2,36,768]{2,1,0:T(8,128)(2,1)S(1)}, bf16[2,36,768]{2,1,0:T(8,128)(2,1)S(1)}, u32[]{:S(2)}, u32[]{:S(2)}) collective-permute-start(bf16[2,36,768]{2,1,0:T(8,128)(2,1)S(1)} %slice.72), channel_id=1, source_target_pairs={{0,1},{1,2},{2,3},{3,4},{4,5},{5,6},{6,7},{7,8},{8,9},{9,10},{10,1... | collective-permute-start | bytes 331784 | tf_op jit(solution)/shard_map/ppermute | solution.py:348
where the time goes:
time: 53 us; the launch traced here: 52.7 us
  Pallas kernels  21.6 us (41%)
  waiting for transfers between devices  12.6 us (24%)
  local copies, waits for them, and re-layouts  6.39 us (12%)
  starting transfers between devices  5.63 us (11%)
  between operations  5.15 us (10%)
  other arithmetic  1.31 us (2%)
    ppermute x4, waiting for transfers between devices, summed(): lax.ppermute(value, axis, [(i, i ^ step) for i in range(size)])  12.6 us
    pallas_call x1, Pallas kernels, pair_bias(): pl.pallas_call(bias_kernel, out_shape=jax.ShapeDtypeStruct((WTYPES, TOK,...  11 us
    pallas_call x1, Pallas kernels, windows(): pl.pallas_call(window_kernel, grid=(count,), out_shape=[jax.ShapeDtypeStr...  10.5 us
    ppermute x1, starting transfers between devices, local(): arrived = lax.ppermute(fields[:, :edge], 'lon', down)  5.5 us
    unnamed x21, local copies, waits for them, and re-layouts  3.17 us
    another operation x1, other arithmetic, local(): return jnp.stack([first, second * jnp.sqrt(total / second_sum)])  1.16 us
  transfers between devices with their start and end apart: 6, of which 4 were waited for; matrix products, arithmetic and copies ran while one was open for 5% of the time, Pallas kernels for 21%

commit v1 on v0

v1 whole, which is shorter than its diff:
```python
import functools

import jax
import jax.numpy as jnp
from jax import lax
from jax.experimental import pallas as pl
from jax.experimental.pallas import tpu as pltpu
from jax.sharding import PartitionSpec as P

C = 192
HEADS = 6
HEAD = 32
WLON = 12
WLAT = 6
WLEV = 2
LEV = 4
ECLS = 3
LAT = 6
WTYPES = 2
NPOS = 3312

HALF = WLON // 2
TOK = WLON * WLAT * WLEV
PLANE = WLON * WLAT
LANE = 128
TAIL = TOK - LANE
WIDE = 2 * LANE
KEYS = (HEADS + 1) * LANE
ROWS = -(-NPOS // LANE)
NEG = -1000000000.0

HI_PAIR = 0
TAIL_AT = WIDE
MAIN_AT = WIDE + LANE
SMALLEST, LARGEST = -2.0, 306.0
STEPS = 65535.0


def main_at(h):
    return MAIN_AT + LANE * h if h < 4 else HI_PAIR + LANE * (h - 4)


def iota(shape, dim):
    return lax.broadcasted_iota(jnp.int32, shape, dim)


def dot(a, b):
    return lax.dot_general(a, b, (((1,), (0,)), ((), ())), preferred_element_type=jnp.float32)


def dot_nt(a, b):
    return lax.dot_general(a, b, (((1,), (1,)), ((), ())), preferred_element_type=jnp.float32)


def dot_tn(a, b):
    return lax.dot_general(a, b, (((0,), (0,)), ((), ())), preferred_element_type=jnp.float32)


def prepare_kernel(region, idx_ref, tab_ref, w_ref, bias_ref, wide_ref, hi_ref, lo_ref, pair_ref):
    weight = w_ref[...].astype(jnp.float32)
    for n in range(3):
        part = jnp.concatenate([weight[:, C * n : C * (n + 1)], jnp.zeros((C, WIDE - C), jnp.float32)], 1)
        wide_ref[:, WIDE * n : WIDE * (n + 1)] = part.astype(jnp.bfloat16)

    step = (LARGEST - SMALLEST) / STEPS

    def steps(value):
        value = jnp.clip((value - SMALLEST) * (1.0 / step), 0.0, STEPS)
        return (value + 0.5).astype(jnp.int32)

    pair_ref[:, NPOS // LANE * LANE :] = jnp.zeros((8, LANE), jnp.int32)
    pair_ref[0:HEADS, 0:NPOS] = steps(tab_ref[:, 0, :]) * 65536 + steps(tab_ref[:, 1, :])

    def values(word):
        top = lax.shift_right_logical(word, 16).astype(jnp.float32)
        low = (word & 65535).astype(jnp.float32)
        return top * step + SMALLEST, low * step + SMALLEST

    row, col = iota((TOK, TOK), 0), iota((TOK, TOK), 1)
    rows = ((row % PLANE) * WLEV + row // PLANE == col).astype(jnp.bfloat16)
    row, col = iota((TOK, WIDE), 0), iota((TOK, WIDE), 1)
    key = jnp.where(col < LANE, col, LANE + col % TAIL)
    cols = ((key % PLANE) * WLEV + key // PLANE == row).astype(jnp.bfloat16)

    def ordered(value):
        value = value.astype(jnp.float32).astype(jnp.bfloat16)
        return dot(dot(rows, value).astype(jnp.bfloat16), cols).astype(jnp.int32)

    idx = idx_ref[...]
    high, low = ordered(idx >> 7), ordered(idx & 127)
    hi_ref[0:TOK, :] = high[:, :LANE]
    lo_ref[0:TOK, :] = low[:, :LANE]
    slot = iota((8, LANE), 1) // TAIL
    for pack in range(-(-TOK // 64)):
        h = jnp.zeros((8, LANE), jnp.int32)
        l = jnp.zeros((8, LANE), jnp.int32)
        for u in range(8):
            at = 64 * pack + 8 * u
            if at < TOK:
                h = jnp.where(slot == u, high[at : at + 8, LANE:], h)
                l = jnp.where(slot == u, low[at : at + 8, LANE:], l)
        hi_ref[TOK + 8 * pack : TOK + 8 * pack + 8, :] = h
        lo_ref[TOK + 8 * pack : TOK + 8 * pack + 8, :] = l

    def gathered(at):
        h, l = hi_ref[pl.ds(at, 8), :], lo_ref[pl.ds(at, 8), :]
        found = [jnp.zeros((8, LANE), jnp.int32) for _ in range(HEADS)]
        for b in range(ROWS):
            here = h == b
            for n in range(HEADS):
                source = jnp.broadcast_to(pair_ref[n : n + 1, LANE * b : LANE * (b + 1)], (8, LANE))
                found[n] = jnp.where(here, jnp.take_along_axis(source, l, axis=1), found[n])
        return [values(f) for f in found]

    def regions(token, t):
        level, lat = token // PLANE, token % WLAT
        found = jnp.zeros(token.shape, jnp.int32)
        for l in range(WLEV):
            for j in range(WLAT):
                found = jnp.where((level == l) & (lat == j), region[WLEV * t + l, j], found)
        return found

    lane = iota((8, LANE), 1)
    key_main = [regions(lane, t) for t in range(WTYPES)]
    key_tail = [regions(LANE + lane % TAIL, t) for t in range(WTYPES)]

    def main_rows(g, _):
        at = pl.multiple_of(g * 8, 8)
        found = gathered(at)
        query = iota((8, LANE), 0) + at
        for t in range(WTYPES):
            ok = regions(query, t) == key_main[t]
            for h in range(HEADS):
                bias_ref[t, pl.ds(at, 8), main_at(h) : main_at(h) + LANE] = jnp.where(ok, found[h][t], NEG)
        return 0

    lax.fori_loop(0, TOK // 8, main_rows, 0)
    for pack in range(-(-TOK // 64)):
        found = gathered(TOK + 8 * pack)
        for u in range(8):
            at = 64 * pack + 8 * u
            if at >= TOK:
                break
            query = iota((8, LANE), 0) + at
            for t in range(WTYPES):
                ok = (regions(query, t) == key_tail[t]) & (slot < HEADS)
                value = jnp.full((8, LANE), NEG, jnp.float32)
                for h in range(HEADS):
                    moved = pltpu.roll(found[h][t], (TAIL * (h - u)) % LANE, 1)
                    value = jnp.where(slot == h, moved, value)
                bias_ref[t, at : at + 8, TAIL_AT:MAIN_AT] = jnp.where(ok, value, NEG)


def window_kernel(classes, x_ref, gain_ref, w_ref, out_w_ref, bias_ref, table_ref, scaled_ref, back_ref, sums_ref):
    f32, bf16 = jnp.float32, jnp.bfloat16

    def padded(row):
        return jnp.concatenate([row, jnp.zeros((row.shape[0], WIDE - C), row.dtype)], 1)

    gain = padded(gain_ref[...])
    wq, wk, wv = (w_ref[:, WIDE * n : WIDE * (n + 1)] for n in range(3))
    wk_t, wv_t = wk.T[:C], wv.T[:C]
    wo = out_w_ref[...]
    wo = jnp.concatenate([wo.astype(f32), jnp.zeros((C, WIDE - C), f32)], 1).astype(bf16)
    scale = HEAD ** (-0.5)
    table = table_ref[...]

    def energy_row(level):
        found = jnp.zeros((1, C), f32)
        for e in range(ECLS):
            found = found + jnp.where(classes[level] == e, table[e : e + 1, :], 0.0)
        return found

    lane = iota((1, LANE), 1)
    extra = lane >= C - LANE
    row, col = iota((WIDE, LANE), 0), iota((WIDE, LANE), 1)
    spread = ((row < C) & (col >= C - LANE) & (col % 32 == row // HEAD)).astype(bf16)
    row, col = iota((4 * LANE, LANE), 0), iota((4 * LANE, LANE), 1)
    marks = ((col >= C - LANE) & (col % 32 == row // LANE)).astype(bf16)

    def by_head(value, ones):
        low, high = value[:, :LANE], value[:, LANE:]
        nothing = jnp.zeros((1, LANE), bf16)
        left, right, left_tail, right_tail = [], [], [], []
        for h in range(HEADS):
            mark = (extra & (lane % 32 == h)).astype(bf16) if ones else nothing
            if h < 4:
                keep = lane // HEAD == h
                left.append(jnp.where(keep, low[:LANE], nothing))
                left_tail.append(jnp.where(keep, low[LANE:], nothing))
                right_tail.append(jnp.broadcast_to(mark, (TAIL, LANE)))
            else:
                keep = lane // HEAD == h - 4
                right.append(jnp.where(keep, high[:LANE], mark))
                right_tail.append(jnp.where(keep, high[LANE:], mark))
        left_tail.append(jnp.zeros((LANE - 4 * TAIL, LANE), bf16))
        right_tail.append(jnp.zeros((LANE - HEADS * TAIL, LANE), bf16))
        return jnp.concatenate(left_tail + left, 0), jnp.concatenate(right + right_tail, 0)

    def against(a, heads, marked):
        left, right = heads
        parts = [
            dot_nt(a[:, LANE:], right[:WIDE]),
            dot_nt(a, jnp.concatenate([left[:LANE], right[WIDE:]], 1)),
        ]
        if marked:
            parts.append(dot_nt(a, jnp.concatenate([left[LANE:], marks], 1)))
        else:
            parts.append(dot_nt(a[:, :LANE], left[LANE:]))
        return jnp.concatenate(parts, 1)

    def mixed(w, *heads):
        left = dot(w[:, TAIL_AT:], jnp.concatenate([h[0] for h in heads], 1))
        right = dot(w[:, :MAIN_AT], jnp.concatenate([h[1] for h in heads], 1))
        found = []
        for n in range(len(heads)):
            at = slice(LANE * n, LANE * (n + 1))
            found.append(jnp.concatenate([left[:, at], right[:, at]], 1))
        return found

    def with_shift(value, product):
        sums = dot(product.astype(bf16), spread)
        top = sums.astype(bf16)
        rest = (sums - top.astype(f32)).astype(bf16)
        last = jnp.where(extra, jnp.where(lane < 96, -top, -rest), value[:, LANE:])
        return jnp.concatenate([value[:, :LANE], last], 1)

    def pair_columns(j):
        return slice(MAIN_AT + WIDE * j, MAIN_AT + WIDE * (j + 1)) if j < 2 else slice(HI_PAIR, WIDE)

    def transposed_product(lefts, ds):
        count = len(lefts)
        main = [[] for _ in lefts]
        for j in range(HEADS // 2):
            stacked = jnp.concatenate([l[64 * j : 64 * j + 64] for l in lefts], 0)
            part = dot(stacked, ds[:, pair_columns(j)])
            for n in range(count):
                main[n] += [part[64 * n : 64 * n + 32, :LANE], part[64 * n + 32 : 64 * n + 64, LANE:]]
        last = dot(jnp.concatenate([l[:C] for l in lefts], 0), ds[:, TAIL_AT:MAIN_AT])
        found = []
        for n in range(count):
            tail = []
            for h in range(HEADS):
                block = last[C * n + HEAD * h : C * n + HEAD * (h + 1)]
                tail.append(pltpu.roll(block, (LANE - TAIL * h) % LANE, 1)[:, :TAIL])
            both = [jnp.concatenate(main[n], 0), jnp.concatenate(tail, 0)]
            found.append(jnp.concatenate(both, 1).astype(bf16))
        return found

    def turned(value):
        return value.astype(f32).T.astype(bf16)

    def mean(value):
        return jnp.sum(value, -1, keepdims=True) * (1.0 / C)

    channel = iota((1, WIDE), 1) < C
    slot = iota((TOK, LANE), 1) // TAIL
    totals = [jnp.zeros((1, WIDE), f32) for _ in range(3)]
    for t in range(WTYPES):

        def tokens(field):
            parts = []
            for l in range(WLEV * t, WLEV * (t + 1)):
                start = C * l // LANE * LANE
                part = x_ref[field, :, start : start + WIDE].astype(f32)
                if start < C * l:
                    part = pltpu.roll(part, WIDE - (C * l - start), 1)
                parts.append(jnp.where(channel, part, 0.0))
            return jnp.concatenate(parts, 0)

        base = tokens(0)
        centered = jnp.where(channel, base - mean(base), 0.0)
        rstd = lax.rsqrt(mean(centered * centered) + 1e-05)
        hat = centered * rstd
        normed = (hat * gain).astype(bf16)[:, :C]
        q, k, v = (dot(normed, w).astype(bf16) for w in (wq, wk, wv))
        k_heads, v_heads = by_head(k, True), by_head(v, True)

        scores = against(q, k_heads, False) * scale + bias_ref[t]
        tails = scores[:, TAIL_AT:MAIN_AT]
        raised = []
        tail_peak = jnp.zeros((TOK, LANE), f32)
        for h in range(HEADS):
            main = scores[:, main_at(h) : main_at(h) + LANE]
            peak = jnp.max(jnp.maximum(main, jnp.where(slot == h, tails, -jnp.inf)), -1, keepdims=True)
            raised.append(jnp.exp(main - peak))
            tail_peak = jnp.where(slot == h, peak, tail_peak)
        tails = jnp.exp(tails - tail_peak)
        tail_inv = jnp.zeros((TOK, LANE), f32)
        for h in range(HEADS):
            inv = 1.0 / jnp.sum(raised[h] + jnp.where(slot == h, tails, 0.0), -1, keepdims=True)
            raised[h] = raised[h] * inv
            tail_inv = jnp.where(slot == h, inv, tail_inv)
        probs = jnp.concatenate(raised[4:] + [tails * tail_inv] + raised[:4], 1)
        weights = probs.astype(bf16)
        probs = probs * scale
        mean_v, mean_k = mixed(weights, v_heads, k_heads)
        q_t = turned(q)

        rows = [energy_row(WLEV * t + l) for l in range(WLEV)]
        energy = jnp.concatenate([jnp.broadcast_to(padded(r), (PLANE, WIDE)) for r in rows], 0)
        inverse = jnp.concatenate([jnp.broadcast_to(padded(1.0 / r), (PLANE, WIDE)) for r in rows], 0)

        def both(value):
            return jnp.concatenate([value, value], 0)

        direction = jnp.concatenate([tokens(1), tokens(2)], 0)
        hat, rstd = both(hat), both(rstd)
        moved = direction - mean(direction) - hat * mean(hat * direction)
        moved = (moved * rstd * gain).astype(bf16)[:, :C]
        dq, dk, dv = (dot(moved, w).astype(bf16) for w in (wq, wk, wv))
        own = [slice(TOK * f, TOK * (f + 1)) for f in range(2)]
        dk_heads = [by_head(dk[o], False) for o in own]
        dv_heads = [by_head(dv[o], False) for o in own]
        mean_d = [mixed(weights, dv_heads[f], dk_heads[f]) for f in range(2)]
        mean_dv = jnp.concatenate([m[0] for m in mean_d], 0)
        mean_dk = jnp.concatenate([m[1] for m in mean_d], 0)
        shifted = with_shift(dq, dq.astype(f32) * both(mean_k) + both(q.astype(f32)) * mean_dk)
        dscores = against(shifted, k_heads, True)
        dscores = dscores + jnp.concatenate([against(q, d, False) for d in dk_heads], 0)
        dweights = (both(probs) * dscores).astype(bf16)
        dblended = (mixed(dweights, v_heads)[0] + mean_dv).astype(bf16)
        image = direction + dot(dblended[:, :C], wo)

        cot = (both(energy) * image).astype(bf16)
        cot = dot_nt(cot[:, :C], out_w_ref[...])
        cot = padded(cot).astype(bf16)
        shifted = with_shift(cot, cot.astype(f32) * both(mean_v))
        cscores = (both(probs) * against(shifted, v_heads, True)).astype(bf16)
        cq = mixed(cscores, k_heads)[0].astype(bf16)
        ck = [transposed_product([q_t], cscores[o])[0] for o in own]
        cv = transposed_product([turned(cot[o]) for o in own], weights)
        turned_part = [dot_tn(ck[f], wk_t) + dot_tn(cv[f], wv_t) for f in range(2)]
        cnormed = padded(dot_nt(cq, wq) + jnp.concatenate(turned_part, 0))
        cnormed = cnormed.astype(bf16).astype(f32) * gain
        back = cnormed - mean(cnormed) - hat * mean(hat * cnormed)
        out = image + back * rstd * both(inverse)
        for f in range(2):
            for l in range(WLEV):
                at = WLEV * t + l
                part = out[TOK * f + PLANE * l : TOK * f + PLANE * (l + 1), :C]
                scaled_ref[f, :, C * at : C * (at + 1)] = part
                back_ref[f, :, C * at : C * (at + 1)] = part[PLANE // 2 :].astype(bf16)
        result = [out[o] for o in own]
        for n, (a, b) in enumerate(((0, 0), (0, 1), (1, 1))):
            totals[n] = totals[n] + jnp.sum(energy * result[a] * result[b], 0, keepdims=True)
    row, found = iota((8, LANE), 0), jnp.zeros((8, LANE), f32)
    for n in range(3):
        found = jnp.where(row == n, jnp.sum(totals[n], -1, keepdims=True), found)
    sums_ref[...] = found


def finish_kernel(total, sums_ref, scaled_ref, back_ref, out_ref):
    sums = sums_ref[...]
    aa, ab, bb = (sums[n : n + 1, :1] for n in range(3))
    first = jnp.sqrt(total / aa)
    second = jnp.sqrt(total / (bb - ab * ab / aa))
    mixing = -ab / aa * second
    edge = back_ref.shape[1]
    for at, ref in ((0, back_ref), (edge, scaled_ref)):
        a = ref[0, :edge, :].astype(jnp.float32)
        b = ref[1, :edge, :].astype(jnp.float32)
        out_ref[at : at + edge, 0, :] = a * first
        out_ref[at : at + edge, 1, :] = b * second + a * mixing


def whole(memory=pltpu.VMEM):
    return pl.BlockSpec(memory_space=memory)


def limit(mib):
    return pltpu.CompilerParams(vmem_limit_bytes=mib * 1024 * 1024)


def prepare(bias_table, bias_index, region, weight):
    packs = TOK + 8 * -(-TOK // 64)
    return pl.pallas_call(
        prepare_kernel,
        out_shape=[
            jax.ShapeDtypeStruct((WTYPES, TOK, KEYS), jnp.float32),
            jax.ShapeDtypeStruct((C, 3 * WIDE), jnp.bfloat16),
        ],
        in_specs=[whole(pltpu.SMEM), whole(), whole(), whole()],
        out_specs=[whole(), whole()],
        scratch_shapes=[pltpu.VMEM((packs, LANE), jnp.int32)] * 2 + [pltpu.VMEM((8, ROWS * LANE), jnp.int32)],
        compiler_params=limit(12),
        cost_estimate=pl.CostEstimate(flops=100000000, bytes_accessed=1400000, transcendentals=0),
        name="prepare",
    )(region.T, bias_index, jnp.transpose(bias_table, (2, 0, 1)), weight)


def window_step(fields, gain, weight, out_weight, bias, energy_table, level_class):
    return pl.pallas_call(
        window_kernel,
        out_shape=[
            jax.ShapeDtypeStruct((2, PLANE, LEV * C), jnp.float32),
            jax.ShapeDtypeStruct((2, PLANE // 2, LEV * C), jnp.bfloat16),
            jax.ShapeDtypeStruct((8, LANE), jnp.float32),
        ],
        in_specs=[whole(pltpu.SMEM)] + [whole()] * 6,
        out_specs=[whole()] * 3,
        compiler_params=limit(24),
        cost_estimate=pl.CostEstimate(flops=2000000000, bytes_accessed=2500000, transcendentals=250000),
        name="window_step",
    )(level_class, fields, gain, weight, out_weight, bias, energy_table)


def finish(total, sums, scaled, back):
    rows = scaled.shape[1]
    return pl.pallas_call(
        functools.partial(finish_kernel, total),
        out_shape=jax.ShapeDtypeStruct((rows, 2, LEV * C), jnp.float32),
        in_specs=[whole()] * 3,
        out_specs=whole(),
        compiler_params=limit(8),
        cost_estimate=pl.CostEstimate(flops=1000000, bytes_accessed=1000000, transcendentals=8),
        name="finish",
    )(sums, scaled, back)


def summed(value, axis):
    size = lax.axis_size(axis)
    if size & (size - 1):
        return lax.psum(value, axis)
    bits = [1 << b for b in range(size.bit_length() - 1)]
    stages = [bits[:1], bits[1:3]] + [[b] for b in bits[3:]]
    for stage in stages:
        offsets = [0]
        for b in stage:
            offsets += [o + b for o in offsets]
        parts = [lax.ppermute(value, axis, [(i, i ^ o) for i in range(size)]) for o in offsets[1:]]
        value = sum(parts, value)
    return value


def local(
    base_state,
    tangents,
    norm_gain,
    qkv_weight,
    out_weight,
    bias_table,
    bias_index,
    region,
    energy_table,
    level_class,
):
    columns = base_state.shape[0]
    size = lax.axis_size("lon")
    up = [(i, (i + 1) % size) for i in range(size)]
    down = [(j, i) for i, j in up]

    def side(start, stop):
        part = jnp.concatenate([base_state[None, start:stop], tangents[:, start:stop]], 0)
        return part.reshape(3, (stop - start) * LAT, LEV * C)

    arrived = lax.ppermute(side(0, HALF), "lon", down)
    bias, weight = prepare(bias_table, bias_index, region, qkv_weight)
    fields = jnp.concatenate([side(HALF, columns), arrived], 1)
    scaled, back, sums = window_step(fields, norm_gain[None], weight, out_weight, bias, energy_table, level_class)
    returned = lax.ppermute(back, "lon", up)
    sums = summed(sums, "lon")
    total = float(columns * size * LAT * LEV * C)
    finished = finish(total, sums, scaled, returned)
    return jnp.transpose(finished.reshape(columns, LAT, 2, LEV * C), (2, 0, 1, 3))


def solution(mesh):
    placed = (
        P(("grp", "lon"), None, None),
        P(None, ("grp", "lon"), None, None),
    ) + (P(),) * 8
    return jax.shard_map(
        local,
        mesh=mesh,
        in_specs=placed,
        out_specs=P(None, ("grp", "lon"), None, None),
        check_vma=False,
    )
```

time: 53 us -> 35.7 us (0.67)
  Pallas kernels: 21.6 us -> 15.4 us
  between operations: 5.15 us -> 0.18 us
  waiting for transfers between devices: 12.6 us -> 7.79 us
  starting transfers between devices: 5.63 us -> 9.4 us
  local copies, waits for them, and re-layouts: 6.39 us -> 2.67 us
  other arithmetic: 1.31 us -> 0.1 us
    pallas_call x2 -> x3, Pallas kernels: 21.6 us -> 15.4 us  [the longest x1 8.06 us: window_step(): pl.pallas_call(window_kernel, out_shape=[jax.ShapeDtypeStruct((2, PLANE,...]
    ppermute x6 -> x7, waiting for transfers between devices: 12.6 us -> 7.79 us  [the longest x5 6.93 us: summed(): lax.ppermute(value, axis, [(i, i ^ o) for i in range(size)])]
    ppermute x6 -> x7, starting transfers between devices: 5.63 us -> 9.4 us  [the longest x1 5.5 us: local(): arrived = lax.ppermute(side(0, HALF), 'lon', down)]
    unnamed x21 -> x18, local copies, waits for them, and re-layouts: 3.17 us -> 1.46 us
    another operation x2 -> x0, other arithmetic: 1.22 us -> none  [the longest x1 1.16 us: local(): return jnp.stack([first, second * jnp.sqrt(total / second_sum)])]
    concatenate x2 -> x4, local copies, waits for them, and re-layouts: 1.02 us -> 0.08 us  [side(): jnp.concatenate([base_state[None, start:stop], tangents[:, start:stop]], 0)]
    reshape x3 -> x0, local copies, waits for them, and re-layouts: 0.9 us -> none  [the longest x1 0.72 us: pair_bias(): jnp.pad(table, ((0, 0), (0, ROWS * LANE - NPOS)))]
    slice x4 -> x2, local copies, waits for them, and re-layouts: 0.75 us -> 1.13 us  [the longest x1 0.97 us: side(): base_state[None, start:stop]]
  transfers between devices with their start and end apart: 6 -> 7, of which waited for: 4 -> 5; matrix products, arithmetic and copies ran while one was open for 5% -> 0% of each run, Pallas kernels for 21% -> 18%
where the time goes in v1:
time: 35.7 us; the launch traced here: 35.5 us
  Pallas kernels  15.4 us (43%)
  starting transfers between devices  9.4 us (26%)
  waiting for transfers between devices  7.79 us (22%)
  local copies, waits for them, and re-layouts  2.67 us (7%)
    pallas_call x1, Pallas kernels, window_step(): pl.pallas_call(window_kernel, out_shape=[jax.ShapeDtypeStruct((2, PLANE,...  8.06 us
    ppermute x5, waiting for transfers between devices, summed(): lax.ppermute(value, axis, [(i, i ^ o) for i in range(size)])  6.93 us
    pallas_call x1, Pallas kernels, prepare(): pl.pallas_call(prepare_kernel, out_shape=[jax.ShapeDtypeStruct((WTYPES, T...  6.38 us
    ppermute x1, starting transfers between devices, local(): arrived = lax.ppermute(side(0, HALF), 'lon', down)  5.5 us
    ppermute x5, starting transfers between devices, summed(): lax.ppermute(value, axis, [(i, i ^ o) for i in range(size)])  3.9 us
    unnamed x18, local copies, waits for them, and re-layouts  1.46 us
    slice x1, local copies, waits for them, and re-layouts, side(): base_state[None, start:stop]  0.97 us
    pallas_call x1, Pallas kernels, finish(): pl.pallas_call(functools.partial(finish_kernel, total), out_shape=jax.Sha...  0.94 us
  transfers between devices with their start and end apart: 7, of which 5 were waited for; matrix products, arithmetic and copies ran while one was open for 0% of the time, Pallas kernels for 18%

profile of v1, /device:TPU:0, one launch (start us, length us, event | category | flops | bytes accessed | tf_op | source)
XLA Modules:
  0.0 35.5 jit_solution(3162429219349264045)
XLA Ops:
  0.0 0.0 copy-start.8
  0.0 1.0 %fusion.1 = (bf16[6,6,768]{2,1,0:T(8,128)(2,1)S(1)}, bf16[6,6,768]{2,1,0:T(8,128)(2,1)S(1)}) fusion(bf16[12,6,768]{2,1,0:T(8,128)(2,1)} %param.10), kind=kLoop, calls=%fused_computation.4 | loop fusion | bytes 221184 | tf_op jit(solution)/shard_map/slice | solution.py:454
  1.0 0.0 copy-done.8
  1.0 0.2 fusion
  1.2 0.0 copy-start.1
  1.2 0.0 copy-start.2
  1.3 0.0 copy-start
  1.3 5.5 %collective-permute-start = (bf16[3,36,768]{2,1,0:T(8,128)(2,1)S(1)}, bf16[3,36,768]{2,1,0:T(8,128)(2,1)S(1)}, u32[]{:S(2)}, u32[]{:S(2)}) collective-permute-start(bf16[3,36,768]{2,1,0:T(8,128)(2,1)S(1)} %pad_maximum_fusion.1), channel_id=1, source_target_pairs={{1,0},{2,1},{3,2},{4,3},{5,4},{6,5},{7,6},{8,7},{9,8},{10,9},{11,1... | collective-permute-start | bytes 497672 | tf_op jit(solution)/shard_map/ppermute | solution.py:457
  6.8 0.0 copy-start.3
  6.8 0.0 copy-done.1
  6.8 0.0 copy-done.2
  6.9 0.0 copy-done
  6.9 0.6 %copy-done.3 = s32[6,4]{0,1:T(4,128)S(1)} copy-done((s32[6,4]{0,1:T(4,128)S(1)}, s32[6,4]{0,1:T(4,128)}, u32[]{:S(2)}) %copy-start.3) | copy-done | bytes 120
  7.5 6.4 %prepare.1 = (f32[2,144,896]{2,1,0:T(8,128)S(1)}, bf16[192,768]{1,0:T(8,128)(2,1)S(1)}) custom-call(s32[4,6]{1,0:T(4,128)S(1)} %bitcast.9, s32[144,144]{1,0:T(8,128)S(1)} %copy-done.2, f32[6,2,3312]{2,1,0:T(2,128)S(1)} %bitcast.8, bf16[192,576]{1,0:T(8,128)(2,1)S(1)} %copy-done), custom_call_target="tpu_custom_call" | custom-call | flops 100000000 | bytes 1400000 | tf_op jit(solution)/shard_map/prepare/pallas_call | solution.py:377
  13.9 0.0 copy-start.4
  13.9 0.0 collective-permute-done
  13.9 0.1 pad_maximum_fusion.x_ref
  14.0 0.0 copy-start.5
  14.0 0.0 copy-start.6
  14.0 0.0 copy-start.7
  14.0 0.8 %copy-done.4 = bf16[192,192]{1,0:T(8,128)(2,1)S(1)} copy-done((bf16[192,192]{1,0:T(8,128)(2,1)S(1)}, bf16[192,192]{1,0:T(8,128)(2,1)}, u32[]{:S(2)}) %copy-start.4) | copy-done | bytes 73752
  14.8 0.0 copy-done.5
  14.8 0.0 copy-done.6
  14.8 0.0 copy-done.7
  14.8 8.1 %window_step.1 = (f32[2,72,768]{2,1,0:T(8,128)S(1)}, bf16[2,36,768]{2,1,0:T(8,128)(2,1)S(1)}, f32[8,128]{1,0:T(8,128)S(1)}) custom-call(s32[4]{0:T(128)S(1)} %copy-done.7, bf16[3,72,768]{2,1,0:T(8,128)(2,1)S(1)} %pad_maximum_fusion.x_ref, f32[1,192]{1,0:T(1,128)S(1)} %bitcast.10, bf16[192,768]{1,0:T(8,128)(2,1)S(1)} %get-tuple-element.10.w_ref, ...), custom_call_target="tpu_custom_call" | custom-call | flops 2000000000 | bytes 2500000 | tf_op jit(solution)/shard_map/window_step/pallas_call | solution.py:393
  22.9 0.1 collective-permute-start.1
  22.9 1.2 %collective-permute-done.1 = f32[8,128]{1,0:T(8,128)S(1)} collective-permute-done((f32[8,128]{1,0:T(8,128)S(1)}, f32[8,128]{1,0:T(8,128)S(1)}, u32[]{:S(2)}, u32[]{:S(2)}) %collective-permute-start.1) | collective-permute-done | bytes 4128 | tf_op jit(solution)/shard_map/ppermute | solution.py:431
  24.1 0.0 collective-permute-start.4
  24.1 0.0 collective-permute-start.3
  24.1 3.5 %collective-permute-start.2 = (f32[8,128]{1,0:T(8,128)S(1)}, f32[8,128]{1,0:T(8,128)S(1)}, u32[]{:S(2)}, u32[]{:S(2)}) collective-permute-start(f32[8,128]{1,0:T(8,128)S(1)} %add.15), channel_id=1, source_target_pairs={{0,2},{1,3},{2,0},{3,1},{4,6},{5,7},{6,4},{7,5},{8,10},{9,11},{10,... | collective-permute-start | bytes 12296 | tf_op jit(solution)/shard_map/ppermute | solution.py:431
  27.6 0.0 collective-permute-start.6
  27.6 1.0 %collective-permute-done.4 = f32[8,128]{1,0:T(8,128)S(1)} collective-permute-done((f32[8,128]{1,0:T(8,128)S(1)}, f32[8,128]{1,0:T(8,128)S(1)}, u32[]{:S(2)}, u32[]{:S(2)}) %collective-permute-start.4) | collective-permute-done | bytes 4128 | tf_op jit(solution)/shard_map/ppermute | solution.py:431
  28.6 0.0 collective-permute-done.3
  28.6 0.6 %collective-permute-done.2 = f32[8,128]{1,0:T(8,128)S(1)} collective-permute-done((f32[8,128]{1,0:T(8,128)S(1)}, f32[8,128]{1,0:T(8,128)S(1)}, u32[]{:S(2)}, u32[]{:S(2)}) %collective-permute-start.2) | collective-permute-done | bytes 4128 | tf_op jit(solution)/shard_map/ppermute | solution.py:431
  29.2 0.4 %collective-permute-start.5 = (f32[8,128]{1,0:T(8,128)S(1)}, f32[8,128]{1,0:T(8,128)S(1)}, u32[]{:S(2)}, u32[]{:S(2)}) collective-permute-start(f32[8,128]{1,0:T(8,128)S(1)} %add_add_fusion), channel_id=1, source_target_pairs={{0,8},{1,9},{2,10},{3,11},{4,12},{5,13},{6,14},{7,15},{8,0},{9,1},... | collective-permute-start | bytes 12296 | tf_op jit(solution)/shard_map/ppermute | solution.py:431
  29.5 4.2 %collective-permute-done.5 = f32[8,128]{1,0:T(8,128)S(1)} collective-permute-done((f32[8,128]{1,0:T(8,128)S(1)}, f32[8,128]{1,0:T(8,128)S(1)}, u32[]{:S(2)}, u32[]{:S(2)}) %collective-permute-start.5) | collective-permute-done | bytes 4128 | tf_op jit(solution)/shard_map/ppermute | solution.py:431
  33.7 0.9 %collective-permute-done.6.back_ref = bf16[2,36,768]{2,1,0:T(8,128)(2,1)S(1)} collective-permute-done((bf16[2,36,768]{2,1,0:T(8,128)(2,1)S(1)}, bf16[2,36,768]{2,1,0:T(8,128)(2,1)S(1)}, u32[]{:S(2)}, u32[]{:S(2)}) %collective-permute-start.6) | collective-permute-done | bytes 110624 | tf_op jit(solution)/shard_map/ppermute | solution.py:461
  34.6 0.9 %finish.1 = f32[72,2,768]{2,1,0:T(2,128)} custom-call(f32[8,128]{1,0:T(8,128)S(1)} %add.19.sums_ref, f32[2,72,768]{2,1,0:T(8,128)S(1)} %get-tuple-element.13.scaled_ref, bf16[2,36,768]{2,1,0:T(8,128)(2,1)S(1)} %collective-permute-done.6.back_ref), custom_call_target="tpu_custom_call" | custom-call | flops 1000000 | bytes 1000000 | tf_op jit(solution)/shard_map/finish/pallas_call | solution.py:410
  (8 shorter events, 0.1 us)
Async XLA Ops:
  0.0 1.0 %copy-start.8 = (bf16[2,12,6,768]{3,0,2,1:T(2,128)(2,1)S(1)}, bf16[2,12,6,768]{3,0,2,1:T(2,128)(2,1)}, u32[]{:S(2)}) copy-start(bf16[2,12,6,768]{3,0,2,1:T(2,128)(2,1)} %param.11) | copy-start | bytes 663556
  1.2 5.6 %copy-start.1 = (f32[2,3312,6]{1,0,2:T(2,128)S(1)}, f32[2,3312,6]{1,0,2:T(2,128)}, u32[]{:S(2)}) copy-start(f32[2,3312,6]{1,0,2:T(2,128)} %param.15) | copy-start | bytes 476932
  1.2 5.6 %copy-start.2 = (s32[144,144]{1,0:T(8,128)S(1)}, s32[144,144]{1,0:T(8,128)}, u32[]{:S(2)}) copy-start(s32[144,144]{1,0:T(8,128)} %idx_ref.1) | copy-start | bytes 248836
  1.3 5.6 %copy-start = (bf16[192,576]{1,0:T(8,128)(2,1)S(1)}, bf16[192,576]{1,0:T(8,128)(2,1)}, u32[]{:S(2)}) copy-start(bf16[192,576]{1,0:T(8,128)(2,1)} %w_ref.1) | copy-start | bytes 663556
  1.3 12.6 %collective-permute-start = (bf16[3,36,768]{2,1,0:T(8,128)(2,1)S(1)}, bf16[3,36,768]{2,1,0:T(8,128)(2,1)S(1)}, u32[]{:S(2)}, u32[]{:S(2)}) collective-permute-start(bf16[3,36,768]{2,1,0:T(8,128)(2,1)S(1)} %pad_maximum_fusion.1), channel_id=1, source_target_pairs={{1,0},{2,1},{3,2},{4,3},{5,4},{6,5},{7,6},{8,7},{9,8},{10,9},{11,1... | collective-permute-start | bytes 497672 | tf_op jit(solution)/shard_map/ppermute | solution.py:457
  6.8 0.7 %copy-start.3 = (s32[6,4]{0,1:T(4,128)S(1)}, s32[6,4]{0,1:T(4,128)}, u32[]{:S(2)}) copy-start(s32[6,4]{0,1:T(4,128)} %param.17) | copy-start | bytes 292
  13.9 0.9 %copy-start.4 = (bf16[192,192]{1,0:T(8,128)(2,1)S(1)}, bf16[192,192]{1,0:T(8,128)(2,1)}, u32[]{:S(2)}) copy-start(bf16[192,192]{1,0:T(8,128)(2,1)} %out_w_ref.1) | copy-start | bytes 221188
  14.0 0.8 %copy-start.5 = (f32[3,192]{1,0:T(4,128)S(1)}, f32[3,192]{1,0:T(4,128)}, u32[]{:S(2)}) copy-start(f32[3,192]{1,0:T(4,128)} %table_ref.1) | copy-start | bytes 6916
  14.0 0.8 %copy-start.6 = (f32[192]{0:T(256)S(1)}, f32[192]{0:T(256)}, u32[]{:S(2)}) copy-start(f32[192]{0:T(256)} %param.12) | copy-start | bytes 2308
  14.0 0.8 %copy-start.7 = (s32[4]{0:T(128)S(1)}, s32[4]{0:T(128)}, u32[]{:S(2)}) copy-start(s32[4]{0:T(128)} %classes.1) | copy-start | bytes 52
  22.9 1.2 %collective-permute-start.1 = (f32[8,128]{1,0:T(8,128)S(1)}, f32[8,128]{1,0:T(8,128)S(1)}, u32[]{:S(2)}, u32[]{:S(2)}) collective-permute-start(f32[8,128]{1,0:T(8,128)S(1)} %get-tuple-element.12), channel_id=1, source_target_pairs={{0,1},{1,0},{2,3},{3,2},{4,5},{5,4},{6,7},{7,6},{8,9},{9,8},{10,11... | collective-permute-start | bytes 12296 | tf_op jit(solution)/shard_map/ppermute | solution.py:431
  24.1 4.5 %collective-permute-start.4 = (f32[8,128]{1,0:T(8,128)S(1)}, f32[8,128]{1,0:T(8,128)S(1)}, u32[]{:S(2)}, u32[]{:S(2)}) collective-permute-start(f32[8,128]{1,0:T(8,128)S(1)} %add.15), channel_id=1, source_target_pairs={{0,6},{1,7},{2,4},{3,5},{4,2},{5,3},{6,0},{7,1},{8,14},{9,15},{10,... | collective-permute-start | bytes 12296 | tf_op jit(solution)/shard_map/ppermute | solution.py:431
  24.1 4.5 %collective-permute-start.3 = (f32[8,128]{1,0:T(8,128)S(1)}, f32[8,128]{1,0:T(8,128)S(1)}, u32[]{:S(2)}, u32[]{:S(2)}) collective-permute-start(f32[8,128]{1,0:T(8,128)S(1)} %add.15), channel_id=1, source_target_pairs={{0,4},{1,5},{2,6},{3,7},{4,0},{5,1},{6,2},{7,3},{8,12},{9,13},{10,... | collective-permute-start | bytes 12296 | tf_op jit(solution)/shard_map/ppermute | solution.py:431
  24.1 5.1 %collective-permute-start.2 = (f32[8,128]{1,0:T(8,128)S(1)}, f32[8,128]{1,0:T(8,128)S(1)}, u32[]{:S(2)}, u32[]{:S(2)}) collective-permute-start(f32[8,128]{1,0:T(8,128)S(1)} %add.15), channel_id=1, source_target_pairs={{0,2},{1,3},{2,0},{3,1},{4,6},{5,7},{6,4},{7,5},{8,10},{9,11},{10,... | collective-permute-start | bytes 12296 | tf_op jit(solution)/shard_map/ppermute | solution.py:431
  27.6 7.0 %collective-permute-start.6 = (bf16[2,36,768]{2,1,0:T(8,128)(2,1)S(1)}, bf16[2,36,768]{2,1,0:T(8,128)(2,1)S(1)}, u32[]{:S(2)}, u32[]{:S(2)}) collective-permute-start(bf16[2,36,768]{2,1,0:T(8,128)(2,1)S(1)} %get-tuple-element.14), channel_id=1, source_target_pairs={{0,1},{1,2},{2,3},{3,4},{4,5},{5,6},{6,7},{7,8},{8,9},{9,10},{10,1... | collective-permute-start | bytes 331784 | tf_op jit(solution)/shard_map/ppermute | solution.py:461
  29.2 4.5 %collective-permute-start.5 = (f32[8,128]{1,0:T(8,128)S(1)}, f32[8,128]{1,0:T(8,128)S(1)}, u32[]{:S(2)}, u32[]{:S(2)}) collective-permute-start(f32[8,128]{1,0:T(8,128)S(1)} %add_add_fusion), channel_id=1, source_target_pairs={{0,8},{1,9},{2,10},{3,11},{4,12},{5,13},{6,14},{7,15},{8,0},{9,1},... | collective-permute-start | bytes 12296 | tf_op jit(solution)/shard_map/ppermute | solution.py:431
